TPU v7x, 512 devices: a whole 4x8x8 slice. The times are simulated.
512 devices in a mesh: gx: 16 (over y, core), gy: 8 (over z), gz: 4 (over x).
Axes of the slice: x: 4, y: 8, z: 8, core: 2. Of those that a mesh axis runs over, the one named last changes fastest.
Arguments:
- noise: float32 [32, 64, 64, 512], P(None, 'gx', 'gy', 'gz'), may hold values from -32 to 32
- basis: float32 [192, 64, 64, 512], P(None, 'gx', 'gy', 'gz'), may hold values from -5 to 5
- conductivity: float32 [64, 64, 512], P('gx', 'gy', 'gz'), may hold values from 0.2 to 2
- reaction: float32 [64, 64, 512], P('gx', 'gy', 'gz'), may hold values from 0.05 to 0.5
Outputs:
- new_block: float32 [32, 64, 64, 512], P(None, 'gx', 'gy', 'gz')
- factor: float32 [32, 32], replicated
- projection: float32 [192, 32], replicated
All inputs are finite; a program needn't handle non-finite values.
Results may differ from a plain program's by a relative error of at most 0.00012.
Values sent between devices are 32-bit elements; how exact they have to be, the bound alone decides.
No kernel may reach another device: no remote copies, remote signals or barrier semaphores. Data moves between devices by JAX's collectives and lax.ppermute only.
A program may use at most 64 MiB of HBM per device.

v0:
```python
import jax
import jax.numpy as jnp
from jax import lax
from jax.sharding import PartitionSpec as P


def padded(value, sides, width):
    for axis, dim in sides:
        size, length = (lax.axis_size(axis), value.shape[dim])
        up = [(i, (i + 1) % size) for i in range(size - 1)]
        down = [(j, i) for i, j in up]
        last = lax.slice_in_dim(value, length - width, length, axis=dim)
        initial = lax.slice_in_dim(value, 0, width, axis=dim)
        before = lax.ppermute(last, axis, up)
        after = lax.ppermute(initial, axis, down)
        value = jnp.concatenate([before, value, after], axis=dim)
    return value


def stencil(field_pad, theta_pad, reaction_core):
    theta_core = theta_pad[1:-1, 1:-1, 1:-1]
    value_core = field_pad[:, 1:-1, 1:-1, 1:-1]
    result = reaction_core * value_core
    diagonal = reaction_core
    offsets = (
        (slice(2, None), slice(1, -1), slice(1, -1)),
        (slice(None, -2), slice(1, -1), slice(1, -1)),
        (slice(1, -1), slice(2, None), slice(1, -1)),
        (slice(1, -1), slice(None, -2), slice(1, -1)),
        (slice(1, -1), slice(1, -1), slice(2, None)),
        (slice(1, -1), slice(1, -1), slice(None, -2)),
    )
    for slicer in offsets:
        face_value = 0.5 * (theta_core + theta_pad[slicer])
        result = result + face_value * (value_core - field_pad[(slice(None),) + slicer])
        diagonal = diagonal + face_value
    return (result, diagonal)


def rim_layer(field):
    return padded(field, (("gx", 1), ("gy", 2), ("gz", 3)), 1)


def shards(noise, basis, conductivity, reaction):
    highest = lax.Precision.HIGHEST
    columns = noise.shape[0]
    span_x, span_y, span_z = (noise.shape[1], noise.shape[2], noise.shape[3])
    cell_total = float(
        span_x * span_y * span_z * lax.axis_size("gx") * lax.axis_size("gy") * lax.axis_size("gz")
    )
    extended = rim_layer(jnp.concatenate([noise, conductivity[None]], axis=0))
    theta_pad = extended[columns]
    first, diagonal = stencil(extended[:columns], theta_pad, reaction)
    image, unused = stencil(rim_layer(first / diagonal), theta_pad, reaction)
    basis_flat = basis.reshape(basis.shape[0], -1)
    image_flat = image.reshape(columns, -1)

    def local_product(left, right):
        return lax.dot_general(left, right, (((1,), (1,)), ((), ())), precision=highest)

    def remove(block, coeff):
        return block - lax.dot_general(
            coeff, basis_flat, (((0,), (0,)), ((), ())), precision=highest
        )

    def project(block):
        return lax.psum(local_product(basis_flat, block), ("gx", "gy", "gz")) / cell_total

    def gram_sum(block):
        return lax.psum(local_product(block, block), ("gx", "gy", "gz")) / cell_total

    coeff_one = project(image_flat)
    image_one = remove(image_flat, coeff_one)
    coeff_two = project(image_one)
    image_two = remove(image_one, coeff_two)
    gram_two = gram_sum(image_two)
    lower_one = jnp.linalg.cholesky(gram_two)
    middle = jax.scipy.linalg.solve_triangular(lower_one, image_two, lower=True)
    lower_two = jnp.linalg.cholesky(gram_sum(middle))
    new_block = jax.scipy.linalg.solve_triangular(lower_two, middle, lower=True)
    factor = jnp.dot(lower_two.T, lower_one.T, precision=highest)
    return (new_block.reshape(noise.shape), factor, coeff_one + coeff_two)


def solution(mesh):
    return jax.shard_map(
        shards,
        mesh=mesh,
        in_specs=(
            P(None, "gx", "gy", "gz"),
            P(None, "gx", "gy", "gz"),
            P("gx", "gy", "gz"),
            P("gx", "gy", "gz"),
        ),
        out_specs=(P(None, "gx", "gy", "gz"), P(), P()),
        check_vma=False,
    )
```

profile of v0, /device:TPU:26, one launch (start us, length us, event | category | flops | bytes accessed | tf_op | source)
XLA Modules:
  0.0 507.7 jit_solution(3330146122280983451)
XLA Ops:
  0.6 1.2 copy_dynamic-update-slice_fusion
  1.8 0.7 copy_dynamic-update-slice_fusion.1
  2.8 1.9 collective-permute-start
  4.7 3.6 collective-permute-start.1
  8.3 0.8 collective-permute-done
  9.1 1.8 collective-permute-done.1
  11.0 4.3 collective-permute-start.2
  15.3 1.3 collective-permute-start.3
  16.6 1.2 collective-permute-done.2
  17.8 4.7 collective-permute-done.3
  22.5 0.7 copy-done.7
  23.2 0.4 pad_maximum_fusion
  23.6 0.4 fusion.92
  24.0 0.6 copy.33
  24.6 2.4 collective-permute-start.5
  27.0 0.6 copy.32
  27.6 3.4 collective-permute-start.4
  31.0 0.8 copy.35
  31.8 1.7 collective-permute-done.4
  33.5 1.5 copy.34
  35.1 0.9 fusion.53
  36.2 5.2 %fusion.36 = f32[32,4,8,128]{3,1,2,0:T(4,128)S(1)} fusion(f32[33,6,10,1]{3,1,2,0:T(8,128)S(1)} %copy.34, f32[33,6,1,128]{3,1,2,0:T(8,128)S(1)} %copy-done.8, f32[33,6,1,128]{3,1,2,0:T(8,128)S(1)} %copy-done.6, f32[33,1,8,128]{3,1,2,0:T(1,128)S(1)} %collective-permute-done.1, f32[33,4,8,128]{3,1,2,0:T(4,128)S(1)} %copy_dynamic-update-slice_fusion.1, ...), kind=kLoop, calls=%fused_computation.56 | loop fusion | flops 4980736 | bytes 2209248 | tf_op jit(solution)/shard_map/div | solution.py:54
  41.6 3.6 collective-permute-start.7
  45.2 2.0 collective-permute-start.6
  47.2 0.7 collective-permute-done.7
  47.9 2.7 collective-permute-done.6
  50.7 4.3 collective-permute-start.9
  55.0 1.3 collective-permute-start.8
  56.3 1.2 collective-permute-done.9
  57.5 5.9 %collective-permute-done.8 = f32[32,6,1,128]{3,1,2,0:T(8,128)S(1)} collective-permute-done((f32[32,6,1,128]{3,1,2,0:T(8,128)S(1)}, f32[32,6,1,128]{3,1,2,0:T(8,128)S(1)}, u32[]{:S(2)}, u32[]{:S(2)}) %collective-permute-start.8) | collective-permute-done | bytes 98336 | tf_op jit(solution)/shard_map/ppermute | solution.py:15
  63.4 0.6 copy-done.9
  64.5 0.4 fusion.93
  64.9 0.5 copy.45
  65.4 1.9 collective-permute-start.10
  67.3 0.5 copy.47
  67.8 4.1 collective-permute-start.11
  71.9 1.6 copy.46
  73.6 1.6 copy.48
  75.2 5.8 %fusion.17 = f32[32,4,8,128]{3,1,2,0:T(4,128)S(1)} fusion(f32[32,4,8,128]{3,1,2,0:T(4,128)} %copy-done.1, f32[32,6,10,1]{3,1,2,0:T(8,128)} %copy.48, f32[32,6,1,128]{3,1,2,0:T(8,128)} %copy-done.9, f32[32,6,1,128]{3,1,2,0:T(8,128)S(1)} %collective-permute-done.9, f32[32,1,8,128]{3,1,2,0:T(1,128)S(1)} %collective-permute-done.6, ...), kind=kLoop, calls=%fused_computation.19 | loop fusion | flops 4849664 | bytes 1637376 | tf_op jit(solution)/shard_map/add | solution.py:35
  81.1 0.8 copy.49
  81.9 4.3 fusion.9
  86.2 100.3 %psum.28 = f32[192,32]{0,1:T(8,128)S(1)} all-reduce(f32[192,32]{0,1:T(8,128)S(1)} %fusion.9), channel_id=1, replica_groups=mesh['gx'=16,'gy'=8,'gz'=4] {'gx','gy','gz'}, use_global_device_ids=true, to_apply=%region_0.0 | all-reduce | flops 6144 | bytes 49152 | tf_op jit(solution)/shard_map/psum | solution.py:67
  186.6 4.8 convolution_subtract_fusion.1
  191.4 0.8 copy-done.3
  192.2 4.0 fusion.12
  196.3 96.0 %psum.29 = f32[192,32]{0,1:T(8,128)S(1)} all-reduce(f32[192,32]{0,1:T(8,128)S(1)} %fusion.12), channel_id=1, replica_groups=mesh['gx'=16,'gy'=8,'gz'=4] {'gx','gy','gz'}, use_global_device_ids=true, to_apply=%region_1.0 | all-reduce | flops 6144 | bytes 49152 | tf_op jit(solution)/shard_map/psum | solution.py:67
  292.3 4.7 convolution_subtract_fusion
  297.0 0.7 multiply_add_fusion
  297.8 0.6 fusion.96
  298.4 94.5 %psum.30 = f32[32,32]{0,1:T(8,128)S(1)} all-reduce(f32[32,32]{0,1:T(8,128)S(1)} %fusion.96), channel_id=1, replica_groups=mesh['gx'=16,'gy'=8,'gz'=4] {'gx','gy','gz'}, use_global_device_ids=true, to_apply=%region_2.0 | all-reduce | flops 1024 | bytes 8192 | tf_op jit(solution)/shard_map/psum | solution.py:70
  393.0 2.9 cholesky.44
  395.9 0.7 compare_reduce_fusion.1
  396.6 0.6 fusion.70
  397.2 2.4 custom-call.6
  399.7 1.7 fusion.64
  401.4 0.6 fusion.97
  401.9 95.4 %psum.31 = f32[32,32]{0,1:T(8,128)S(1)} all-reduce(f32[32,32]{0,1:T(8,128)S(1)} %fusion.97), channel_id=1, replica_groups=mesh['gx'=16,'gy'=8,'gz'=4] {'gx','gy','gz'}, use_global_device_ids=true, to_apply=%region_5.8 | all-reduce | flops 1024 | bytes 8192 | tf_op jit(solution)/shard_map/psum | solution.py:70
  497.4 2.9 cholesky.55
  500.4 0.6 compare_reduce_fusion
  501.0 2.1 fusion.75
  503.1 0.7 select_bitcast_fusion
  503.8 2.4 custom-call.7
  506.2 0.7 convolution_bitcast_fusion
  506.9 0.9 copy.61
  (48 shorter events, 1.6 us)
Async XLA Ops:
  2.8 6.3 %collective-permute-start = (f32[33,1,8,128]{3,1,2,0:T(1,128)S(1)}, f32[33,1,8,128]{3,1,2,0:T(1,128)S(1)}, u32[]{:S(2)}, u32[]{:S(2)}) collective-permute-start(f32[33,1,8,128]{3,1,2,0:T(1,128)S(1)} %get-tuple-element.20), channel_id=1, source_target_pairs={{0,32},{32,64},{64,96},{96,128},{128,160},{160,192},{192,224},{224... | collective-permute-start | bytes 405512 | tf_op jit(solution)/shard_map/ppermute | solution.py:14
  4.7 6.2 %collective-permute-start.1 = (f32[33,1,8,128]{3,1,2,0:T(1,128)S(1)}, f32[33,1,8,128]{3,1,2,0:T(1,128)S(1)}, u32[]{:S(2)}, u32[]{:S(2)}) collective-permute-start(f32[33,1,8,128]{3,1,2,0:T(1,128)S(1)} %get-tuple-element.21), channel_id=1, source_target_pairs={{32,0},{64,32},{96,64},{128,96},{160,128},{192,160},{224,192},{256... | collective-permute-start | bytes 405512 | tf_op jit(solution)/shard_map/ppermute | solution.py:15
  11.0 6.8 %collective-permute-start.2 = (f32[33,6,1,128]{3,1,2,0:T(8,128)S(1)}, f32[33,6,1,128]{3,1,2,0:T(8,128)S(1)}, u32[]{:S(2)}, u32[]{:S(2)}) collective-permute-start(f32[33,6,1,128]{3,1,2,0:T(8,128)S(1)} %get-tuple-element.16), channel_id=1, source_target_pairs={{0,4},{4,8},{8,12},{12,16},{16,20},{20,24},{24,28},{1,5},{5,9},{9,... | collective-permute-start | bytes 304136 | tf_op jit(solution)/shard_map/ppermute | solution.py:14
  15.3 7.3 %collective-permute-start.3 = (f32[33,6,1,128]{3,1,2,0:T(8,128)S(1)}, f32[33,6,1,128]{3,1,2,0:T(8,128)S(1)}, u32[]{:S(2)}, u32[]{:S(2)}) collective-permute-start(f32[33,6,1,128]{3,1,2,0:T(8,128)S(1)} %get-tuple-element.17), channel_id=1, source_target_pairs={{4,0},{8,4},{12,8},{16,12},{20,16},{24,20},{28,24},{5,1},{9,5},{13... | collective-permute-start | bytes 304136 | tf_op jit(solution)/shard_map/ppermute | solution.py:15
  17.8 4.7 copy-start.5
  22.5 0.7 copy-start.7
  24.6 6.4 %collective-permute-start.5 = (f32[33,6,10,1]{0,3,2,1:T(1,128)S(1)}, f32[33,6,10,1]{0,3,2,1:T(1,128)S(1)}, u32[]{:S(2)}, u32[]{:S(2)}) collective-permute-start(f32[33,6,10,1]{0,3,2,1:T(1,128)S(1)} %copy.33), channel_id=1, source_target_pairs={{1,0},{2,1},{3,2},{5,4},{6,5},{7,6},{9,8},{10,9},{11,10},{13,12},{... | collective-permute-start | bytes 23768 | tf_op jit(solution)/shard_map/ppermute | solution.py:15
  27.6 5.9 %collective-permute-start.4 = (f32[33,6,10,1]{0,3,2,1:T(1,128)S(1)}, f32[33,6,10,1]{0,3,2,1:T(1,128)}, u32[]{:S(2)}, u32[]{:S(2)}) collective-permute-start(f32[33,6,10,1]{0,3,2,1:T(1,128)S(1)} %copy.32), channel_id=1, source_target_pairs={{0,1},{1,2},{2,3},{4,5},{5,6},{6,7},{8,9},{9,10},{10,11},{12,13},{... | collective-permute-start | bytes 23768 | tf_op jit(solution)/shard_map/ppermute | solution.py:14
  35.0 1.0 copy-start.16
  35.0 1.1 copy-start.4
  35.0 1.1 copy-start.6
  35.0 1.1 copy-start.8
  36.1 5.3 %copy-start.10 = (f32[4,8,128]{2,0,1:T(4,128)}, f32[4,8,128]{2,0,1:T(4,128)S(1)}, u32[]{:S(2)}) copy-start(f32[4,8,128]{2,0,1:T(4,128)S(1)} %get-tuple-element.7) | copy-start | bytes 49156
  36.1 5.3 %copy-start.11 = (f32[4,8,128]{2,0,1:T(4,128)}, f32[4,8,128]{2,0,1:T(4,128)S(1)}, u32[]{:S(2)}) copy-start(f32[4,8,128]{2,0,1:T(4,128)S(1)} %get-tuple-element.8) | copy-start | bytes 49156
  36.1 5.3 %copy-start.12 = (f32[4,8,128]{2,0,1:T(4,128)}, f32[4,8,128]{2,0,1:T(4,128)S(1)}, u32[]{:S(2)}) copy-start(f32[4,8,128]{2,0,1:T(4,128)S(1)} %get-tuple-element.9) | copy-start | bytes 49156
  36.1 5.3 %copy-start.13 = (f32[4,8,128]{2,0,1:T(4,128)}, f32[4,8,128]{2,0,1:T(4,128)S(1)}, u32[]{:S(2)}) copy-start(f32[4,8,128]{2,0,1:T(4,128)S(1)} %get-tuple-element.10) | copy-start | bytes 49156
  36.1 5.3 %copy-start.14 = (f32[4,8,128]{2,0,1:T(4,128)}, f32[4,8,128]{2,0,1:T(4,128)S(1)}, u32[]{:S(2)}) copy-start(f32[4,8,128]{2,0,1:T(4,128)S(1)} %get-tuple-element.11) | copy-start | bytes 49156
  36.2 5.3 %copy-start.15 = (f32[4,8,128]{2,0,1:T(4,128)}, f32[4,8,128]{2,0,1:T(4,128)S(1)}, u32[]{:S(2)}) copy-start(f32[4,8,128]{2,0,1:T(4,128)S(1)} %get-tuple-element.24) | copy-start | bytes 49156
  41.4 22.0 %copy-start.1 = (f32[32,4,8,128]{3,1,2,0:T(4,128)}, f32[32,4,8,128]{3,1,2,0:T(4,128)S(1)}, u32[]{:S(2)}) copy-start(f32[32,4,8,128]{3,1,2,0:T(4,128)S(1)} %fusion.36) | copy-start | bytes 1572868
  41.6 6.3 %collective-permute-start.7 = (f32[32,1,8,128]{3,1,2,0:T(1,128)S(1)}, f32[32,1,8,128]{3,1,2,0:T(1,128)S(1)}, u32[]{:S(2)}, u32[]{:S(2)}) collective-permute-start(f32[32,1,8,128]{3,1,2,0:T(1,128)S(1)} %get-tuple-element.22), channel_id=1, source_target_pairs={{0,32},{32,64},{64,96},{96,128},{128,160},{160,192},{192,224},{224... | collective-permute-start | bytes 393224 | tf_op jit(solution)/shard_map/ppermute | solution.py:14
  45.2 5.4 %collective-permute-start.6 = (f32[32,1,8,128]{3,1,2,0:T(1,128)S(1)}, f32[32,1,8,128]{3,1,2,0:T(1,128)S(1)}, u32[]{:S(2)}, u32[]{:S(2)}) collective-permute-start(f32[32,1,8,128]{3,1,2,0:T(1,128)S(1)} %get-tuple-element.23), channel_id=1, source_target_pairs={{32,0},{64,32},{96,64},{128,96},{160,128},{192,160},{224,192},{256... | collective-permute-start | bytes 393224 | tf_op jit(solution)/shard_map/ppermute | solution.py:15
  50.7 6.8 %collective-permute-start.9 = (f32[32,6,1,128]{3,1,2,0:T(8,128)S(1)}, f32[32,6,1,128]{3,1,2,0:T(8,128)S(1)}, u32[]{:S(2)}, u32[]{:S(2)}) collective-permute-start(f32[32,6,1,128]{3,1,2,0:T(8,128)S(1)} %get-tuple-element.18), channel_id=1, source_target_pairs={{0,4},{4,8},{8,12},{12,16},{16,20},{20,24},{24,28},{1,5},{5,9},{9,... | collective-permute-start | bytes 294920 | tf_op jit(solution)/shard_map/ppermute | solution.py:14
  55.0 8.4 %collective-permute-start.8 = (f32[32,6,1,128]{3,1,2,0:T(8,128)S(1)}, f32[32,6,1,128]{3,1,2,0:T(8,128)S(1)}, u32[]{:S(2)}, u32[]{:S(2)}) collective-permute-start(f32[32,6,1,128]{3,1,2,0:T(8,128)S(1)} %get-tuple-element.19), channel_id=1, source_target_pairs={{4,0},{8,4},{12,8},{16,12},{20,16},{24,20},{28,24},{5,1},{9,5},{13... | collective-permute-start | bytes 294920 | tf_op jit(solution)/shard_map/ppermute | solution.py:15
  63.4 0.6 copy-start.9
  65.4 6.5 %collective-permute-start.10 = (f32[32,6,10,1]{0,3,2,1:T(1,128)S(1)}, f32[32,6,10,1]{0,3,2,1:T(1,128)S(1)}, u32[]{:S(2)}, u32[]{:S(2)}) collective-permute-start(f32[32,6,10,1]{0,3,2,1:T(1,128)S(1)} %copy.45), channel_id=1, source_target_pairs={{1,0},{2,1},{3,2},{5,4},{6,5},{7,6},{9,8},{10,9},{11,10},{13,12},{... | collective-permute-start | bytes 23048 | tf_op jit(solution)/shard_map/ppermute | solution.py:15
  67.8 5.8 %collective-permute-start.11 = (f32[32,6,10,1]{0,3,2,1:T(1,128)S(1)}, f32[32,6,10,1]{0,3,2,1:T(1,128)S(1)}, u32[]{:S(2)}, u32[]{:S(2)}) collective-permute-start(f32[32,6,10,1]{0,3,2,1:T(1,128)S(1)} %copy.47), channel_id=1, source_target_pairs={{0,1},{1,2},{2,3},{4,5},{5,6},{6,7},{8,9},{9,10},{10,11},{12,13},{... | collective-permute-start | bytes 23048 | tf_op jit(solution)/shard_map/ppermute | solution.py:14
  75.2 6.7 %copy-start = (f32[192,4,8,128]{3,2,1,0:T(8,128)S(1)}, f32[192,4,8,128]{3,2,1,0:T(8,128)}, u32[]{:S(2)}) copy-start(f32[192,4,8,128]{3,2,1,0:T(8,128)} %param.8) | copy-start | bytes 9437188
  191.4 0.8 copy-start.3
  297.0 0.8 copy-start.2
where the time goes:
time: 509 us; the launch traced here: 508 us
  blocking collectives  386 us (76%)
  starting transfers between devices  34.1 us (7%)
  other arithmetic  27 us (5%)
  matrix products  23.4 us (5%)
  waiting for transfers between devices  20.8 us (4%)
  local copies, waits for them, and re-layouts  15 us (3%)
    psum x2, blocking collectives, project(): lax.psum(local_product(basis_flat, block), ('gx', 'gy', 'gz')) / cell_total  196 us
    psum x2, blocking collectives, gram_sum(): lax.psum(local_product(block, block), ('gx', 'gy', 'gz')) / cell_total  190 us
    ppermute x6, starting transfers between devices, padded(): before = lax.ppermute(last, axis, up)  21.5 us
    ppermute x6, waiting for transfers between devices, padded(): after = lax.ppermute(initial, axis, down)  15.1 us
    ppermute x6, starting transfers between devices, padded(): after = lax.ppermute(initial, axis, down)  12.6 us
  transfers between devices with their start and end apart: 12, of which 9 were waited for; matrix products, arithmetic and copies ran while one was open for 1% of the time, Pallas kernels for 0%

commit v1 on v0

--- a/solution.py
+++ b/solution.py
@@ -67,7 +67,10 @@
         return lax.psum(local_product(basis_flat, block), ("gx", "gy", "gz")) / cell_total
 
     def gram_sum(block):
-        return lax.psum(local_product(block, block), ("gx", "gy", "gz")) / cell_total
+        place_turns_all = lambda panel: lax.psum(
+            lax.psum(panel, axis_name=("gy", "gz")), axis_name="gx"
+        )
+        return place_turns_all(local_product(block, block)) / cell_total
 
     coeff_one = project(image_flat)
     image_one = remove(image_flat, coeff_one)

time: 509 us -> 687 us (1.35)
  the two profiles are of different devices: /device:TPU:26 before, /device:TPU:32 now
where the time goes in v1:
time: 687 us; the launch traced here: 686 us
  blocking collectives  563 us (82%)
  starting transfers between devices  37.5 us (5%)
  other arithmetic  27.1 us (4%)
  matrix products  23.5 us (3%)
  waiting for transfers between devices  18.7 us (3%)
  local copies, waits for them, and re-layouts  15.1 us (2%)
    psum x2, blocking collectives, gram_sum(): lax.psum(panel, axis_name=('gy', 'gz'))  278 us
    psum x2, blocking collectives, project(): lax.psum(local_product(basis_flat, block), ('gx', 'gy', 'gz')) / cell_total  193 us
    psum x2, blocking collectives, gram_sum(): lax.psum(lax.psum(panel, axis_name=('gy', 'gz')), axis_name='gx')  91.5 us
    ppermute x6, starting transfers between devices, padded(): before = lax.ppermute(last, axis, up)  22.7 us
    ppermute x6, starting transfers between devices, padded(): after = lax.ppermute(initial, axis, down)  14.9 us
    ppermute x6, waiting for transfers between devices, padded(): after = lax.ppermute(initial, axis, down)  14.3 us
  transfers between devices with their start and end apart: 12, of which 9 were waited for; matrix products, arithmetic and copies ran while one was open for 1% of the time, Pallas kernels for 0%

profile of v1, /device:TPU:32, one launch (start us, length us, event | category | flops | bytes accessed | tf_op | source)
XLA Modules:
  0.0 686.2 jit_solution(9755889342452332826)
XLA Ops:
  0.6 1.2 copy_dynamic-update-slice_fusion
  1.8 0.7 copy_dynamic-update-slice_fusion.1
  2.8 1.9 collective-permute-start
  4.7 4.9 collective-permute-start.1
  9.6 0.8 collective-permute-done
  10.3 1.8 collective-permute-done.1
  12.2 4.3 collective-permute-start.2
  16.5 1.3 collective-permute-start.3
  17.8 1.4 collective-permute-done.2
  19.2 4.8 collective-permute-done.3
  23.9 0.7 copy-done.7
  25.0 0.4 fusion.92
  25.4 0.6 copy.33
  26.0 1.3 collective-permute-start.5
  27.3 0.6 copy.32
  27.9 5.1 collective-permute-start.4
  33.0 0.8 copy.35
  34.0 1.5 copy.34
  35.5 0.9 fusion.53
  36.7 5.2 fusion.36
  42.1 1.9 collective-permute-start.7
  44.0 4.9 collective-permute-start.6
  48.9 0.7 collective-permute-done.7
  49.6 1.8 collective-permute-done.6
  51.5 4.3 collective-permute-start.9
  55.8 1.3 collective-permute-start.8
  57.1 1.3 collective-permute-done.9
  58.4 6.0 collective-permute-done.8
  64.4 0.7 copy-done.9
  65.4 0.4 fusion.93
  65.8 0.5 copy.45
  66.3 1.3 collective-permute-start.10
  67.6 0.5 copy.47
  68.2 5.1 collective-permute-start.11
  73.3 1.6 copy.46
  74.9 1.6 copy.48
  76.6 5.8 fusion.17
  82.4 0.8 copy.49
  83.2 4.3 fusion.9
  87.6 98.6 %psum.42 = f32[192,32]{0,1:T(8,128)S(1)} all-reduce(f32[192,32]{0,1:T(8,128)S(1)} %fusion.9), channel_id=1, replica_groups=mesh['gx'=16,'gy'=8,'gz'=4] {'gx','gy','gz'}, use_global_device_ids=true, to_apply=%region_0.0 | all-reduce | flops 6144 | bytes 49152 | tf_op jit(solution)/shard_map/psum | solution.py:67
  186.1 4.8 convolution_subtract_fusion.1
  191.0 0.8 copy-done.3
  191.8 4.0 fusion.12
  195.8 94.7 %psum.43 = f32[192,32]{0,1:T(8,128)S(1)} all-reduce(f32[192,32]{0,1:T(8,128)S(1)} %fusion.12), channel_id=1, replica_groups=mesh['gx'=16,'gy'=8,'gz'=4] {'gx','gy','gz'}, use_global_device_ids=true, to_apply=%region_1.0 | all-reduce | flops 6144 | bytes 49152 | tf_op jit(solution)/shard_map/psum | solution.py:67
  290.5 4.7 convolution_subtract_fusion
  295.3 0.7 multiply_add_fusion
  296.1 0.6 fusion.96
  296.6 140.8 %psum.44 = f32[32,32]{0,1:T(8,128)S(1)} all-reduce(f32[32,32]{0,1:T(8,128)S(1)} %fusion.96), channel_id=1, replica_groups=mesh['gx'=16,'gy'=8,'gz'=4] {'gy','gz'}, use_global_device_ids=true, to_apply=%region_2.0 | all-reduce | flops 1024 | bytes 8192 | tf_op jit(solution)/shard_map/psum | solution.py:71
  437.4 45.7 %psum.45 = f32[32,32]{0,1:T(8,128)S(1)} all-reduce(f32[32,32]{0,1:T(8,128)S(1)} %psum.44), channel_id=1, replica_groups=mesh['gx'=16,'gy'=8,'gz'=4] {'gx'}, use_global_device_ids=true, to_apply=%region_3.0 | all-reduce | flops 1024 | bytes 8192 | tf_op jit(solution)/shard_map/psum | solution.py:70
  483.3 2.9 cholesky.44
  486.2 0.7 compare_reduce_fusion.1
  486.9 0.7 fusion.70
  487.6 2.4 custom-call.6
  490.1 1.7 fusion.64
  491.8 0.6 fusion.97
  492.3 137.7 %psum.46 = f32[32,32]{0,1:T(8,128)S(1)} all-reduce(f32[32,32]{0,1:T(8,128)S(1)} %fusion.97), channel_id=1, replica_groups=mesh['gx'=16,'gy'=8,'gz'=4] {'gy','gz'}, use_global_device_ids=true, to_apply=%region_6.9 | all-reduce | flops 1024 | bytes 8192 | tf_op jit(solution)/shard_map/psum | solution.py:71
  630.0 45.7 %psum.47 = f32[32,32]{0,1:T(8,128)S(1)} all-reduce(f32[32,32]{0,1:T(8,128)S(1)} %psum.46), channel_id=1, replica_groups=mesh['gx'=16,'gy'=8,'gz'=4] {'gx'}, use_global_device_ids=true, to_apply=%region_7.10 | all-reduce | flops 1024 | bytes 8192 | tf_op jit(solution)/shard_map/psum | solution.py:70
  675.8 2.9 cholesky.55
  678.8 0.6 compare_reduce_fusion
  679.4 2.2 fusion.75
  681.6 0.7 select_bitcast_fusion
  682.2 2.4 custom-call.7
  684.7 0.7 convolution_bitcast_fusion
  685.3 0.9 copy.61
  (50 shorter events, 2.1 us)
Async XLA Ops:
  2.8 7.5 %collective-permute-start = (f32[33,1,8,128]{3,1,2,0:T(1,128)S(1)}, f32[33,1,8,128]{3,1,2,0:T(1,128)S(1)}, u32[]{:S(2)}, u32[]{:S(2)}) collective-permute-start(f32[33,1,8,128]{3,1,2,0:T(1,128)S(1)} %get-tuple-element.20), channel_id=1, source_target_pairs={{0,32},{32,64},{64,96},{96,128},{128,160},{160,192},{192,224},{224... | collective-permute-start | bytes 405512 | tf_op jit(solution)/shard_map/ppermute | solution.py:14
  4.7 7.4 %collective-permute-start.1 = (f32[33,1,8,128]{3,1,2,0:T(1,128)S(1)}, f32[33,1,8,128]{3,1,2,0:T(1,128)S(1)}, u32[]{:S(2)}, u32[]{:S(2)}) collective-permute-start(f32[33,1,8,128]{3,1,2,0:T(1,128)S(1)} %get-tuple-element.21), channel_id=1, source_target_pairs={{32,0},{64,32},{96,64},{128,96},{160,128},{192,160},{224,192},{256... | collective-permute-start | bytes 405512 | tf_op jit(solution)/shard_map/ppermute | solution.py:15
  12.2 7.0 %collective-permute-start.2 = (f32[33,6,1,128]{3,1,2,0:T(8,128)S(1)}, f32[33,6,1,128]{3,1,2,0:T(8,128)S(1)}, u32[]{:S(2)}, u32[]{:S(2)}) collective-permute-start(f32[33,6,1,128]{3,1,2,0:T(8,128)S(1)} %get-tuple-element.16), channel_id=1, source_target_pairs={{0,4},{4,8},{8,12},{12,16},{16,20},{20,24},{24,28},{1,5},{5,9},{9,... | collective-permute-start | bytes 304136 | tf_op jit(solution)/shard_map/ppermute | solution.py:14
  16.5 7.5 %collective-permute-start.3 = (f32[33,6,1,128]{3,1,2,0:T(8,128)S(1)}, f32[33,6,1,128]{3,1,2,0:T(8,128)S(1)}, u32[]{:S(2)}, u32[]{:S(2)}) collective-permute-start(f32[33,6,1,128]{3,1,2,0:T(8,128)S(1)} %get-tuple-element.17), channel_id=1, source_target_pairs={{4,0},{8,4},{12,8},{16,12},{20,16},{24,20},{28,24},{5,1},{9,5},{13... | collective-permute-start | bytes 304136 | tf_op jit(solution)/shard_map/ppermute | solution.py:15
  19.2 4.8 copy-start.5
  23.9 0.7 copy-start.7
  26.0 7.0 %collective-permute-start.5 = (f32[33,6,10,1]{0,3,2,1:T(1,128)S(1)}, f32[33,6,10,1]{0,3,2,1:T(1,128)S(1)}, u32[]{:S(2)}, u32[]{:S(2)}) collective-permute-start(f32[33,6,10,1]{0,3,2,1:T(1,128)S(1)} %copy.33), channel_id=1, source_target_pairs={{1,0},{2,1},{3,2},{5,4},{6,5},{7,6},{9,8},{10,9},{11,10},{13,12},{... | collective-permute-start | bytes 23768 | tf_op jit(solution)/shard_map/ppermute | solution.py:15
  27.9 6.1 collective-permute-start.4
  35.5 1.0 copy-start.16
  35.5 1.1 copy-start.4
  35.5 1.1 copy-start.6
  35.5 1.1 copy-start.8
  36.6 5.3 copy-start.10
  36.6 5.3 copy-start.11
  36.6 5.3 copy-start.12
  36.6 5.3 copy-start.13
  36.6 5.3 copy-start.14
  36.6 5.3 copy-start.15
  41.9 22.5 %copy-start.1 = (f32[32,4,8,128]{3,1,2,0:T(4,128)}, f32[32,4,8,128]{3,1,2,0:T(4,128)S(1)}, u32[]{:S(2)}) copy-start(f32[32,4,8,128]{3,1,2,0:T(4,128)S(1)} %fusion.36) | copy-start | bytes 1572868
  42.1 7.5 %collective-permute-start.7 = (f32[32,1,8,128]{3,1,2,0:T(1,128)S(1)}, f32[32,1,8,128]{3,1,2,0:T(1,128)S(1)}, u32[]{:S(2)}, u32[]{:S(2)}) collective-permute-start(f32[32,1,8,128]{3,1,2,0:T(1,128)S(1)} %get-tuple-element.22), channel_id=1, source_target_pairs={{0,32},{32,64},{64,96},{96,128},{128,160},{160,192},{192,224},{224... | collective-permute-start | bytes 393224 | tf_op jit(solution)/shard_map/ppermute | solution.py:14
  44.0 7.4 %collective-permute-start.6 = (f32[32,1,8,128]{3,1,2,0:T(1,128)S(1)}, f32[32,1,8,128]{3,1,2,0:T(1,128)S(1)}, u32[]{:S(2)}, u32[]{:S(2)}) collective-permute-start(f32[32,1,8,128]{3,1,2,0:T(1,128)S(1)} %get-tuple-element.23), channel_id=1, source_target_pairs={{32,0},{64,32},{96,64},{128,96},{160,128},{192,160},{224,192},{256... | collective-permute-start | bytes 393224 | tf_op jit(solution)/shard_map/ppermute | solution.py:15
  51.5 6.9 %collective-permute-start.9 = (f32[32,6,1,128]{3,1,2,0:T(8,128)S(1)}, f32[32,6,1,128]{3,1,2,0:T(8,128)S(1)}, u32[]{:S(2)}, u32[]{:S(2)}) collective-permute-start(f32[32,6,1,128]{3,1,2,0:T(8,128)S(1)} %get-tuple-element.18), channel_id=1, source_target_pairs={{0,4},{4,8},{8,12},{12,16},{16,20},{20,24},{24,28},{1,5},{5,9},{9,... | collective-permute-start | bytes 294920 | tf_op jit(solution)/shard_map/ppermute | solution.py:14
  55.8 8.6 %collective-permute-start.8 = (f32[32,6,1,128]{3,1,2,0:T(8,128)S(1)}, f32[32,6,1,128]{3,1,2,0:T(8,128)S(1)}, u32[]{:S(2)}, u32[]{:S(2)}) collective-permute-start(f32[32,6,1,128]{3,1,2,0:T(8,128)S(1)} %get-tuple-element.19), channel_id=1, source_target_pairs={{4,0},{8,4},{12,8},{16,12},{20,16},{24,20},{28,24},{5,1},{9,5},{13... | collective-permute-start | bytes 294920 | tf_op jit(solution)/shard_map/ppermute | solution.py:15
  64.4 0.7 copy-start.9
  66.3 6.9 %collective-permute-start.10 = (f32[32,6,10,1]{0,3,2,1:T(1,128)S(1)}, f32[32,6,10,1]{0,3,2,1:T(1,128)S(1)}, u32[]{:S(2)}, u32[]{:S(2)}) collective-permute-start(f32[32,6,10,1]{0,3,2,1:T(1,128)S(1)} %copy.45), channel_id=1, source_target_pairs={{1,0},{2,1},{3,2},{5,4},{6,5},{7,6},{9,8},{10,9},{11,10},{13,12},{... | collective-permute-start | bytes 23048 | tf_op jit(solution)/shard_map/ppermute | solution.py:15
  68.2 6.8 collective-permute-start.11
  76.6 6.7 copy-start
  191.0 0.8 copy-start.3
  295.3 0.8 copy-start.2
